TPU v7x, 512 devices: a whole 4x8x8 slice. The times are simulated.
512 devices in a mesh: ctx: 32 (over y, x), db: 16 (over z, core).
Axes of the slice: x: 4, y: 8, z: 8, core: 2. Of those that a mesh axis runs over, the one named last changes fastest.
Arguments:
- stream: bfloat16 [12288, 4096], P('ctx', 'db'), may hold values from -6 to 6
- history: bfloat16 [8, 12288, 4096], P(None, 'ctx', 'db'), may hold values from -6 to 6
- dwa_weights: float32 [9], replicated, may hold values from -0.5 to 1
- w_query: bfloat16 [4096, 4096], P('ctx', 'db'), may hold values from -0.09375 to 0.09375
- w_out: bfloat16 [4096, 4096], P('db', 'ctx'), may hold values from -0.1875 to 0.1875
- encoded_kv: bfloat16 [16, 24, 128, 2, 4096], P('db', None, 'ctx'), may hold values from -340 to 340
- neighbour_ids: int32 [384], replicated, may hold values from 0 to 383, each once
Outputs:
- block_out: bfloat16 [12288, 4096], P('ctx', 'db')
- dense: bfloat16 [12288, 4096], P('ctx', 'db')
Inputs may be any that keep to these rules, and one draw needn't show every extreme that they name: `neighbour_ids`: each stored neighbour is named by exactly one slot.
All inputs are finite; a program needn't handle non-finite values.
Results may differ from a plain program's by a relative error of at most 0.014.
The roundings to bfloat16 on the way count: a program that leaves them out, or rounds other values in their place, can miss the bound.
Values may be sent and summed in bfloat16 or wider, within the bound.
No kernel may reach another device: no remote copies, remote signals or barrier semaphores. Data moves between devices by JAX's collectives and lax.ppermute only.
A program may use at most 64 MiB of HBM per device.

v0:
```python
import jax
import jax.numpy as jnp
from jax import lax
from jax.sharding import PartitionSpec as P

HDIM = 128
SPAN = 64
NNB = 2


def shifted(block, axis, distance):
    devices = range(lax.axis_size(axis))
    route = [(i - distance, i) for i in devices if i - distance in devices]
    return lax.ppermute(block, axis, route)


def attend(queries, key_rows, value_rows):
    group_count, row_count, width = queries.shape
    head_count = width // HDIM
    query_heads = queries.reshape(group_count, row_count, head_count, HDIM)
    key_heads = key_rows.reshape(group_count, key_rows.shape[1], head_count, HDIM)
    value_heads = value_rows.reshape(group_count, value_rows.shape[1], head_count, HDIM)
    scores = jnp.einsum(
        "gqhd,gkhd->ghqk", query_heads, key_heads, preferred_element_type=jnp.float32
    ) * HDIM ** (-0.5)
    row_max = jnp.max(scores, axis=-1, keepdims=True)
    exponent = jnp.exp(scores - row_max)
    weights = (exponent / jnp.sum(exponent, axis=-1, keepdims=True)).astype(jnp.bfloat16)
    mixed = jnp.einsum("ghqk,gkhd->gqhd", weights, value_heads, preferred_element_type=jnp.float32)
    return mixed.astype(jnp.bfloat16).reshape(group_count, row_count, width)


def on_device(stream, history, dwa_weights, w_query, w_out, encoded_kv, neighbour_ids):
    tok_rows = stream.shape[0]
    local_width = w_query.shape[1]
    spans_here = tok_rows // SPAN
    lead_rows = SPAN - 1
    full_stream = lax.all_gather(stream, "db", axis=1, tiled=True)
    queries = jnp.dot(
        full_stream,
        lax.all_gather(w_query, "ctx", axis=0, tiled=True),
        preferred_element_type=jnp.float32,
    ).astype(jnp.bfloat16)
    out_full = lax.all_gather(w_out, "ctx", axis=1, tiled=True)
    groups_here = lax.all_to_all(encoded_kv, "db", split_axis=4, concat_axis=0, tiled=True)
    slab_rows = encoded_kv.shape[2]
    store = groups_here.reshape(-1, slab_rows, 2, local_width)
    ctx_count = lax.axis_size("ctx")
    row_requests = neighbour_ids.shape[0] // ctx_count
    wanted = neighbour_ids.reshape(ctx_count, row_requests).T
    outgoing = jnp.take(store, wanted, axis=0)
    arrived = lax.all_to_all(outgoing, "ctx", split_axis=1, concat_axis=1, tiled=True)
    neighbours = arrived.reshape(spans_here, NNB * ctx_count * slab_rows, 2, local_width)
    key_rows = neighbours[:, :, 0]
    value_rows = neighbours[:, :, 1]
    carried = shifted(neighbours[spans_here - 1], "ctx", 1)
    all_keys = jnp.concatenate([carried[None, :, 0], key_rows], 0)
    all_values = jnp.concatenate([carried[None, :, 1], value_rows], 0)
    padded = jnp.concatenate(
        [
            jnp.zeros((1, local_width), jnp.bfloat16),
            queries,
            jnp.zeros((lead_rows, local_width), jnp.bfloat16),
        ],
        0,
    )
    padded = padded.reshape(spans_here + 1, SPAN, local_width)
    mixed = attend(padded, all_keys, all_values).reshape(-1, local_width)
    attended = mixed[1 : tok_rows + 1]
    partial_value = jnp.dot(attended, out_full, preferred_element_type=jnp.float32)
    summed = lax.psum_scatter(
        partial_value.astype(jnp.bfloat16), "db", scatter_dimension=1, tiled=True
    ).astype(jnp.float32)
    block = stream.astype(jnp.float32) + summed
    dense = dwa_weights[-1] * block + jnp.sum(
        history.astype(jnp.float32) * dwa_weights[:-1, None, None], axis=0
    )
    return (block.astype(jnp.bfloat16), dense.astype(jnp.bfloat16))


def solution(mesh):
    placed = (
        P("ctx", "db"),
        P(None, "ctx", "db"),
        P(),
        P("ctx", "db"),
        P("db", "ctx"),
        P("db", None, "ctx", None, None),
        P(),
    )
    return jax.shard_map(
        on_device,
        mesh=mesh,
        in_specs=placed,
        out_specs=(P("ctx", "db"), P("ctx", "db")),
        check_vma=False,
    )
```

profile of v0, /device:TPU:4, one launch (start us, length us, event | category | flops | bytes accessed | tf_op | source)
XLA Modules:
  0.0 305.9 jit_solution(4108286600987173053)
XLA Ops:
  7.2 0.0 all-gather.6.cloned.1.call-start
  7.2 0.7 all-gather.6.cloned.1.call-update
  7.9 0.0 all-gather.4.cloned.1.call-start
  7.9 0.7 all-gather.4.cloned.1.call-update
  8.6 13.2 %copy.54 = bf16[1,24,4,2,4096]{1,2,3,0,4:T(4,128)(2,1)} copy(bf16[1,24,4,2,4096]{4,3,2,1,0:T(2,128)(2,1)} %param.12) | data formatting | bytes 3145728 | tf_op args[5]
  21.8 12.7 %reshape.48 = bf16[16,2,24576]{2,1,0:T(2,128)(2,1)} reshape(bf16[4096,1,2,4,24]{4,3,2,1,0:T(4,128)(2,1)} %bitcast.32) | data formatting | bytes 3145728
  34.6 0.0 copy-start.3
  34.6 10.6 %all-to-all-start = ((bf16[16,2,24576]{2,1,0:T(2,128)(2,1)}), bf16[16,2,24576]{2,1,0:T(2,128)(2,1)S(1)}, u32[]{:S(2)}, u32[]{:S(2)}) async-start(bf16[16,2,24576]{2,1,0:T(2,128)(2,1)} %reshape.48), calls=%async_computation | async-start | bytes 3145728 | tf_op jit(solution)/shard_map/all_to_all | solution.py:45
  45.1 0.0 copy-done.3
  45.1 0.1 reshape.34
  45.3 0.1 copy.57
  45.3 0.1 reshape.39
  45.5 37.5 %all-to-all-done = bf16[16,2,24576]{2,1,0:T(2,128)(2,1)S(1)} async-done(((bf16[16,2,24576]{2,1,0:T(2,128)(2,1)}), bf16[16,2,24576]{2,1,0:T(2,128)(2,1)S(1)}, u32[]{:S(2)}, u32[]{:S(2)}) %all-to-all-start) | async-done | bytes 1572896 | tf_op jit(solution)/shard_map/all_to_all | solution.py:45
  83.0 12.9 %reshape.49 = bf16[4096,1,2,4,24]{4,3,2,1,0:T(4,128)(2,1)} reshape(bf16[16,2,24576]{2,1,0:T(2,128)(2,1)S(1)} %all-to-all-done) | data formatting | bytes 3145728
  95.8 10.8 %copy.73 = bf16[1,24,4,2,16,256]{5,1,4,3,2,0:T(8,128)(2,1)S(1)} copy(bf16[1,24,4,2,16,256]{1,2,3,5,4,0:T(4,128)(2,1)} %bitcast.31) | data formatting | bytes 3145728 | tf_op jit(solution)/shard_map/all_to_all | solution.py:45
  106.6 1.2 copy.58
  107.9 3.2 %gather_fusion = bf16[384,4,2,256]{3,1,2,0:T(4,128)(2,1)S(1)} fusion(bf16[384,4,2,256]{3,1,2,0:T(4,128)(2,1)S(1)} %copy.58, s32[1024]{0:T(1024)S(1)} %pad_clamp_fusion), kind=kCustom, calls=%fused_computation | custom fusion | bytes 3147264 | tf_op jit(solution)/shard_map/jit(_take)/gather | solution.py:51
  111.0 3.0 broadcast_select_fusion
  114.0 10.2 %all-to-all-start.1 = ((bf16[12,32,4,2,256]{4,3,2,0,1:T(2,128)(2,1)}), bf16[12,32,4,2,256]{4,3,2,0,1:T(2,128)(2,1)S(1)}, u32[]{:S(2)}, u32[]{:S(2)}) async-start(bf16[12,32,4,2,256]{4,3,2,0,1:T(2,128)(2,1)} %broadcast_select_fusion), calls=%async_computation.1 | async-start | bytes 3145728 | tf_op jit(solution)/shard_map/all_to_all | solution.py:52
  124.2 0.0 all-gather.8.cloned.1.call-start
  124.3 0.7 all-gather.8.cloned.1.call-update
  125.0 0.0 reduce-scatter.2.cloned.1.call-start
  125.0 0.1 pad.6.clone
  125.1 0.0 all-gather.6.cloned.1.call-done
  125.1 21.3 %all-gather.4.cloned.1.call-done = bf16[384,4096]{1,0:T(8,128)(2,1)} async-done(((bf16[384,256]{1,0:T(8,128)(2,1)}), bf16[384,4096]{1,0:T(8,128)(2,1)}) %all-gather.4.cloned.1.call-update) | async-done | bytes 3145744 | tf_op jit(solution)/shard_map/all_gather | solution.py:38
  146.4 3.5 %convolution_convert_fusion.2 = bf16[384,256]{1,0:T(8,128)(2,1)S(1)} fusion(bf16[384,4096]{1,0:T(8,128)(2,1)} %all-gather.4.cloned.1.call-done, bf16[4096,256]{1,0:T(8,128)(2,1)} %all-gather.6.cloned.1.call-done), kind=kOutput, calls=%fused_computation.9 | convolution fusion | flops 805404672 | bytes 5439488 | tf_op jit(solution)/shard_map/dot_general | solution.py:39
  149.9 0.2 maximum_maximum_fusion
  150.1 0.8 reshape_reshape.6
  150.9 14.0 %all-to-all-done.1 = bf16[12,32,4,2,256]{4,3,2,0,1:T(2,128)(2,1)S(1)} async-done(((bf16[12,32,4,2,256]{4,3,2,0,1:T(2,128)(2,1)}), bf16[12,32,4,2,256]{4,3,2,0,1:T(2,128)(2,1)S(1)}, u32[]{:S(2)}, u32[]{:S(2)}) %all-to-all-start.1) | async-done | bytes 1572896 | tf_op jit(solution)/shard_map/all_to_all | solution.py:52
  164.9 0.2 slice.35
  165.1 0.9 copy.60
  166.0 2.1 collective-permute-start
  168.1 1.3 copy.62
  169.5 2.2 fusion.28
  171.7 2.6 copy.67
  174.3 1.5 copy.69
  175.8 0.9 copy.63
  176.7 0.4 copy.65
  177.1 0.0 copy-start.2
  177.1 0.0 collective-permute-done
  177.1 0.4 fusion.29
  177.5 0.1 copy.66
  177.6 0.1 copy.68
  177.8 0.1 copy.61
  177.9 0.1 copy.64
  178.0 0.0 copy-done.2
  178.0 1.5 fusion.30
  179.5 1.5 fusion.3
  181.0 0.2 copy.71
  181.3 46.6 %all-gather.8.cloned.1.call-done = bf16[256,4096]{1,0:T(8,128)(2,1)} async-done(((bf16[256,128]{1,0:T(8,128)(2,1)}), bf16[256,4096]{1,0:T(8,128)(2,1)}) %all-gather.8.cloned.1.call-update) | async-done | bytes 2097168 | tf_op jit(solution)/shard_map/all_gather | solution.py:44
  228.0 4.2 %convolution_convert_fusion = bf16[384,4096]{1,0:T(8,128)(2,1)} fusion(bf16[256,4096]{1,0:T(8,128)(2,1)} %all-gather.8.cloned.1.call-done, bf16[448,256]{1,0:T(8,128)(2,1)S(1)} %bitcast.38), kind=kOutput, calls=%fused_computation.2 | convolution fusion | flops 806879232 | bytes 5439488 | tf_op jit(solution)/shard_map/dot_general | solution.py:70
  232.2 0.0 copy-start.4
  232.2 0.0 copy-start
  232.2 0.0 reduce-scatter.2.cloned.1.call-update
  232.2 0.6 copy-done.4
  232.8 0.0 copy-start.1
  232.8 0.6 slice.31
  233.4 0.2 copy-done
  233.6 0.4 multiply_reduce_fusion
  234.0 63.0 %reduce-scatter.2.cloned.1.call-done = bf16[384,256]{1,0:T(8,128)(2,1)} async-done(((bf16[384,4096]{1,0:T(8,128)(2,1)}), bf16[384,256]{1,0:T(8,128)(2,1)}) %reduce-scatter.2.cloned.1.call-update) | async-done | bytes 196624 | tf_op jit(solution)/shard_map/reduce_scatter | solution.py:71
  297.0 0.0 copy-done.1
  297.0 2.4 add_convert_fusion
  (6 shorter events, 0.1 us)
Async XLA Ops:
  7.2 118.0 %all-gather.6.cloned.1.call-start = ((), (), s32[]{:S(2)}) async-start(), calls=%async_computation.4 | async-start | bytes 2162688 | tf_op jit(solution)/shard_map/all_gather | solution.py:41
  7.9 138.5 %all-gather.4.cloned.1.call-start = ((), (), s32[]{:S(2)}) async-start(), calls=%async_computation.3 | async-start | bytes 3342336 | tf_op jit(solution)/shard_map/all_gather | solution.py:38
  34.6 10.6 %copy-start.3 = (s32[384]{0:T(512)S(1)}, s32[384]{0:T(512)}, u32[]{:S(2)}) copy-start(s32[384]{0:T(512)} %param.13) | copy-start | bytes 4612
  34.6 48.4 %all-to-all-start = ((bf16[16,2,24576]{2,1,0:T(2,128)(2,1)}), bf16[16,2,24576]{2,1,0:T(2,128)(2,1)S(1)}, u32[]{:S(2)}, u32[]{:S(2)}) async-start(bf16[16,2,24576]{2,1,0:T(2,128)(2,1)} %reshape.48), calls=%async_computation | async-start | bytes 3145728 | tf_op jit(solution)/shard_map/all_to_all | solution.py:45
  114.0 50.9 %all-to-all-start.1 = ((bf16[12,32,4,2,256]{4,3,2,0,1:T(2,128)(2,1)}), bf16[12,32,4,2,256]{4,3,2,0,1:T(2,128)(2,1)S(1)}, u32[]{:S(2)}, u32[]{:S(2)}) async-start(bf16[12,32,4,2,256]{4,3,2,0,1:T(2,128)(2,1)} %broadcast_select_fusion), calls=%async_computation.1 | async-start | bytes 3145728 | tf_op jit(solution)/shard_map/all_to_all | solution.py:52
  124.2 103.7 %all-gather.8.cloned.1.call-start = ((), (), s32[]{:S(2)}) async-start(), calls=%async_computation.5 | async-start | bytes 2162688 | tf_op jit(solution)/shard_map/all_gather | solution.py:44
  125.0 172.0 %reduce-scatter.2.cloned.1.call-start = ((), (), s32[]{:S(2)}) async-start(), calls=%async_computation.6 | async-start | bytes 3342336 | tf_op jit(solution)/shard_map/reduce_scatter | solution.py:71
  166.0 11.1 %collective-permute-start = (bf16[256,2,256]{2,1,0:T(2,128)(2,1)}, bf16[256,2,256]{2,1,0:T(2,128)(2,1)S(1)}, u32[]{:S(2)}, u32[]{:S(2)}) collective-permute-start(bf16[256,2,256]{2,1,0:T(2,128)(2,1)} %bitcast.6), channel_id=1, source_target_pairs={{0,16},{16,32},{32,48},{48,64},{64,80},{80,96},{96,112},{112,128},... | collective-permute-start | bytes 786440 | tf_op jit(solution)/shard_map/ppermute | solution.py:14
  177.1 0.9 copy-start.2
  232.2 0.7 copy-start.4
  232.2 1.4 copy-start
  232.8 64.2 %copy-start.1 = (bf16[384,256]{1,0:T(8,128)(2,1)S(1)}, bf16[384,256]{1,0:T(8,128)(2,1)}, u32[]{:S(2)}) copy-start(bf16[384,256]{1,0:T(8,128)(2,1)} %param.7) | copy-start | bytes 589828
Sparse Core Ops, SparseCore 0:
  11.1 86.3 all-gather.5
  99.6 46.7 all-gather.3
  149.4 78.4 all-gather.7
  232.3 64.6 reduce-scatter.1
where the time goes:
time: 307 us; the launch traced here: 306 us
  waiting for transfers between devices  185 us (60%)
  local copies, waits for them, and re-layouts  67.7 us (22%)
  starting transfers between devices  23.1 us (8%)
  between operations  14 us (5%)
  matrix products  10.7 us (3%)
  other arithmetic  5.92 us (2%)
    reduce_scatter x1, waiting for transfers between devices, on_device(): lax.psum_scatter(partial_value.astype(jnp.bfloat16), 'db', scatter_dimens...  63 us
    all_gather x1, waiting for transfers between devices, on_device(): out_full = lax.all_gather(w_out, 'ctx', axis=1, tiled=True)  46.6 us
    unnamed x14, local copies, waits for them, and re-layouts  39.6 us
    all_to_all x1, waiting for transfers between devices, on_device(): lax.all_to_all(encoded_kv, 'db', split_axis=4, concat_axis=0, tiled=True)  37.5 us
    all_gather x1, waiting for transfers between devices, on_device(): full_stream = lax.all_gather(stream, 'db', axis=1, tiled=True)  21.3 us
    all_to_all x1, waiting for transfers between devices, on_device(): lax.all_to_all(outgoing, 'ctx', split_axis=1, concat_axis=1, tiled=True)  14 us
    all_to_all x1, local copies, waits for them, and re-layouts, on_device(): lax.all_to_all(encoded_kv, 'db', split_axis=4, concat_axis=0, tiled=True)  10.8 us
    all_to_all x1, starting transfers between devices, on_device(): lax.all_to_all(encoded_kv, 'db', split_axis=4, concat_axis=0, tiled=True)  10.6 us
  transfers between devices with their start and end apart: 7, of which 5 were waited for; matrix products, arithmetic and copies ran while one was open for 25% of the time, Pallas kernels for 0%

commit v1 on v0

--- a/solution.py
+++ b/solution.py
@@ -35,7 +35,9 @@
     local_width = w_query.shape[1]
     spans_here = tok_rows // SPAN
     lead_rows = SPAN - 1
-    full_stream = lax.all_gather(stream, "db", axis=1, tiled=True)
+    full_stream = jnp.concatenate(
+        lax.all_to_all(jnp.stack([stream] * lax.axis_size("db")), "db", 0, 0), axis=1
+    )
     queries = jnp.dot(
         full_stream,
         lax.all_gather(w_query, "ctx", axis=0, tiled=True),

time: 307 us -> 343 us (1.12)
  waiting for transfers between devices: 185 us -> 211 us
  starting transfers between devices: 23.1 us -> 29.4 us
    all_to_all x0 -> x1, waiting for transfers between devices: none -> 39.8 us  [on_device(): lax.all_to_all(jnp.stack([stream] * lax.axis_size('db')), 'db', 0, 0)]
    all_gather x1 -> x0, waiting for transfers between devices: 21.3 us -> none  [on_device(): full_stream = lax.all_gather(stream, 'db', axis=1, tiled=True)]
    all_to_all x1, waiting for transfers between devices: 14 us -> 27.4 us  [on_device(): lax.all_to_all(outgoing, 'ctx', split_axis=1, concat_axis=1, tiled=True)]
    all_gather x1, waiting for transfers between devices: 46.6 us -> 36 us  [on_device(): out_full = lax.all_gather(w_out, 'ctx', axis=1, tiled=True)]
    all_gather x1, waiting for transfers between devices: 0.01 us -> 6.08 us  [on_device(): lax.all_gather(w_query, 'ctx', axis=0, tiled=True)]
    all_to_all x0 -> x1, starting transfers between devices: none -> 4.97 us  [on_device(): lax.all_to_all(jnp.stack([stream] * lax.axis_size('db')), 'db', 0, 0)]
    unnamed x14 -> x17, local copies, waits for them, and re-layouts: 39.6 us -> 39.8 us
  transfers between devices with their start and end apart: 7 -> 7, of which waited for: 5 -> 6; matrix products, arithmetic and copies ran while one was open for 25% -> 15% of each run, Pallas kernels for 0% -> 0%
where the time goes in v1:
time: 343 us; the launch traced here: 341 us
  waiting for transfers between devices  211 us (62%)
  local copies, waits for them, and re-layouts  70 us (20%)
  starting transfers between devices  29.4 us (9%)
  between operations  14 us (4%)
  matrix products  10.8 us (3%)
  other arithmetic  5.92 us (2%)
    reduce_scatter x1, waiting for transfers between devices, on_device(): lax.psum_scatter(partial_value.astype(jnp.bfloat16), 'db', scatter_dimens...  63 us
    unnamed x17, local copies, waits for them, and re-layouts  39.8 us
    all_to_all x1, waiting for transfers between devices, on_device(): lax.all_to_all(jnp.stack([stream] * lax.axis_size('db')), 'db', 0, 0)  39.8 us
    all_to_all x1, waiting for transfers between devices, on_device(): lax.all_to_all(encoded_kv, 'db', split_axis=4, concat_axis=0, tiled=True)  37.7 us
    all_gather x1, waiting for transfers between devices, on_device(): out_full = lax.all_gather(w_out, 'ctx', axis=1, tiled=True)  36 us
    all_to_all x1, waiting for transfers between devices, on_device(): lax.all_to_all(outgoing, 'ctx', split_axis=1, concat_axis=1, tiled=True)  27.4 us
    all_to_all x1, local copies, waits for them, and re-layouts, on_device(): lax.all_to_all(encoded_kv, 'db', split_axis=4, concat_axis=0, tiled=True)  10.8 us
    all_to_all x1, starting transfers between devices, on_device(): lax.all_to_all(encoded_kv, 'db', split_axis=4, concat_axis=0, tiled=True)  10.6 us
  transfers between devices with their start and end apart: 7, of which 6 were waited for; matrix products, arithmetic and copies ran while one was open for 15% of the time, Pallas kernels for 0%

profile of v1, /device:TPU:4, one launch (start us, length us, event | category | flops | bytes accessed | tf_op | source)
XLA Modules:
  0.0 341.4 jit_solution(18300394118482292368)
XLA Ops:
  7.2 13.2 %copy.57 = bf16[1,24,4,2,4096]{1,2,3,0,4:T(4,128)(2,1)} copy(bf16[1,24,4,2,4096]{4,3,2,1,0:T(2,128)(2,1)} %param.12) | data formatting | bytes 3145728 | tf_op args[5]
  20.4 12.7 %reshape.58 = bf16[16,2,24576]{2,1,0:T(2,128)(2,1)} reshape(bf16[4096,1,2,4,24]{4,3,2,1,0:T(4,128)(2,1)} %bitcast.35) | data formatting | bytes 3145728
  33.1 0.0 copy-start.1
  33.1 10.6 %all-to-all-start = ((bf16[16,2,24576]{2,1,0:T(2,128)(2,1)}), bf16[16,2,24576]{2,1,0:T(2,128)(2,1)S(1)}, u32[]{:S(2)}, u32[]{:S(2)}) async-start(bf16[16,2,24576]{2,1,0:T(2,128)(2,1)} %reshape.58), calls=%async_computation | async-start | bytes 3145728 | tf_op jit(solution)/shard_map/all_to_all | solution.py:47
  43.6 0.0 copy-done.1
  43.6 0.2 copy.69
  43.8 37.7 %all-to-all-done = bf16[16,2,24576]{2,1,0:T(2,128)(2,1)S(1)} async-done(((bf16[16,2,24576]{2,1,0:T(2,128)(2,1)}), bf16[16,2,24576]{2,1,0:T(2,128)(2,1)S(1)}, u32[]{:S(2)}, u32[]{:S(2)}) %all-to-all-start) | async-done | bytes 1572896 | tf_op jit(solution)/shard_map/all_to_all | solution.py:47
  81.5 2.1 stack.2
  83.6 0.0 copy-start.4
  83.6 5.0 %all-to-all-start.2 = ((bf16[16,384,256]{1,2,0:T(8,128)(2,1)}), bf16[16,384,256]{1,2,0:T(8,128)(2,1)}, u32[]{:S(2)}, u32[]{:S(2)}) async-start(bf16[16,384,256]{1,2,0:T(8,128)(2,1)} %stack.2), calls=%async_computation.2 | async-start | bytes 6291456 | tf_op jit(solution)/shard_map/all_to_all | solution.py:39
  88.6 0.0 all-gather.3.cloned.1.call-start
  88.7 0.7 all-gather.3.cloned.1.call-update
  89.4 0.0 copy-done.4
  89.4 0.1 reshape.42
  89.5 0.1 copy.60
  89.6 0.1 reshape.49
  89.7 12.9 %reshape.59 = bf16[4096,1,2,4,24]{4,3,2,1,0:T(4,128)(2,1)} reshape(bf16[16,2,24576]{2,1,0:T(2,128)(2,1)S(1)} %all-to-all-done) | data formatting | bytes 3145728
  102.5 10.8 %copy.77 = bf16[1,24,4,2,16,256]{5,1,4,3,2,0:T(8,128)(2,1)S(1)} copy(bf16[1,24,4,2,16,256]{1,2,3,5,4,0:T(4,128)(2,1)} %bitcast.34) | data formatting | bytes 3145728 | tf_op jit(solution)/shard_map/all_to_all | solution.py:47
  113.4 1.2 copy.61
  114.6 3.2 gather_fusion
  117.7 3.0 broadcast_select_fusion
  120.7 39.8 %all-to-all-done.2 = bf16[16,384,256]{1,2,0:T(8,128)(2,1)} async-done(((bf16[16,384,256]{1,2,0:T(8,128)(2,1)}), bf16[16,384,256]{1,2,0:T(8,128)(2,1)}, u32[]{:S(2)}, u32[]{:S(2)}) %all-to-all-start.2) | async-done | bytes 3145760 | tf_op jit(solution)/shard_map/all_to_all | solution.py:39
  160.5 10.2 %all-to-all-start.1 = ((bf16[12,32,4,2,256]{4,3,2,0,1:T(2,128)(2,1)}), bf16[12,32,4,2,256]{4,3,2,0,1:T(2,128)(2,1)S(1)}, u32[]{:S(2)}, u32[]{:S(2)}) async-start(bf16[12,32,4,2,256]{4,3,2,0,1:T(2,128)(2,1)} %broadcast_select_fusion), calls=%async_computation.1 | async-start | bytes 3145728 | tf_op jit(solution)/shard_map/all_to_all | solution.py:54
  170.7 0.0 all-gather.5.cloned.1.call-start
  170.8 0.7 all-gather.5.cloned.1.call-update
  171.5 0.0 reduce-scatter.2.cloned.1.call-start
  171.5 0.1 pad.6.clone
  171.6 6.1 %all-gather.3.cloned.1.call-done = bf16[4096,256]{1,0:T(8,128)(2,1)} async-done(((bf16[128,256]{1,0:T(8,128)(2,1)}), bf16[4096,256]{1,0:T(8,128)(2,1)}) %all-gather.3.cloned.1.call-update) | async-done | bytes 2097168 | tf_op jit(solution)/shard_map/all_gather | solution.py:43
  177.7 3.6 %convolution_convert_fusion.2 = bf16[384,256]{1,0:T(8,128)(2,1)S(1)} fusion(bf16[384,4096]{0,1:T(8,128)(2,1)} %bitcast.11, bf16[4096,256]{1,0:T(8,128)(2,1)} %all-gather.3.cloned.1.call-done), kind=kOutput, calls=%fused_computation.9 | convolution fusion | flops 805404672 | bytes 5439488 | tf_op jit(solution)/shard_map/dot_general | solution.py:41
  181.3 0.2 maximum_maximum_fusion
  181.4 0.8 reshape_reshape.6
  182.2 27.4 %all-to-all-done.1 = bf16[12,32,4,2,256]{4,3,2,0,1:T(2,128)(2,1)S(1)} async-done(((bf16[12,32,4,2,256]{4,3,2,0,1:T(2,128)(2,1)}), bf16[12,32,4,2,256]{4,3,2,0,1:T(2,128)(2,1)S(1)}, u32[]{:S(2)}, u32[]{:S(2)}) %all-to-all-start.1) | async-done | bytes 1572896 | tf_op jit(solution)/shard_map/all_to_all | solution.py:54
  209.7 0.2 slice.35
  209.8 0.9 copy.63
  210.7 3.5 %collective-permute-start = (bf16[256,2,256]{2,1,0:T(2,128)(2,1)}, bf16[256,2,256]{2,1,0:T(2,128)(2,1)S(1)}, u32[]{:S(2)}, u32[]{:S(2)}) collective-permute-start(bf16[256,2,256]{2,1,0:T(2,128)(2,1)} %bitcast.6), channel_id=1, source_target_pairs={{0,16},{16,32},{32,48},{48,64},{64,80},{80,96},{96,112},{112,128},... | collective-permute-start | bytes 786440 | tf_op jit(solution)/shard_map/ppermute | solution.py:14
  214.3 1.3 copy.65
  215.6 2.2 fusion.28
  217.9 2.6 copy.71
  220.4 1.5 copy.73
  221.9 0.9 copy.66
  222.9 0.4 copy.68
  223.2 0.0 copy-start.3
  223.3 0.0 collective-permute-done
  223.3 0.4 fusion.29
  223.6 0.1 copy.70
  223.8 0.1 copy.72
  223.9 0.1 copy.64
  224.1 0.1 copy.67
  224.2 0.0 copy-done.3
  224.2 1.5 fusion.30
  225.7 1.5 fusion.3
  227.2 0.2 copy.75
  227.5 36.0 %all-gather.5.cloned.1.call-done = bf16[256,4096]{1,0:T(8,128)(2,1)} async-done(((bf16[256,128]{1,0:T(8,128)(2,1)}), bf16[256,4096]{1,0:T(8,128)(2,1)}) %all-gather.5.cloned.1.call-update) | async-done | bytes 2097168 | tf_op jit(solution)/shard_map/all_gather | solution.py:46
  263.5 4.2 %convolution_convert_fusion = bf16[384,4096]{1,0:T(8,128)(2,1)} fusion(bf16[256,4096]{1,0:T(8,128)(2,1)} %all-gather.5.cloned.1.call-done, bf16[448,256]{1,0:T(8,128)(2,1)S(1)} %bitcast.41), kind=kOutput, calls=%fused_computation.2 | convolution fusion | flops 806879232 | bytes 5439488 | tf_op jit(solution)/shard_map/dot_general | solution.py:72
  267.7 0.0 copy-start.5
  267.7 0.0 copy-start
  267.7 0.0 reduce-scatter.2.cloned.1.call-update
  267.7 0.6 copy-done.5
  268.3 0.6 slice.31
  268.9 0.2 copy-done
  269.1 0.4 multiply_reduce_fusion
  269.5 63.0 %reduce-scatter.2.cloned.1.call-done = bf16[384,256]{1,0:T(8,128)(2,1)} async-done(((bf16[384,4096]{1,0:T(8,128)(2,1)}), bf16[384,256]{1,0:T(8,128)(2,1)}) %reduce-scatter.2.cloned.1.call-update) | async-done | bytes 196624 | tf_op jit(solution)/shard_map/reduce_scatter | solution.py:73
  332.5 0.0 copy-done.2
  332.5 2.4 add_convert_fusion
  (7 shorter events, 0.1 us)
Async XLA Ops:
  33.1 10.6 %copy-start.1 = (bf16[384,256]{1,0:T(8,128)(2,1)S(1)}, bf16[384,256]{1,0:T(8,128)(2,1)}, u32[]{:S(2)}) copy-start(bf16[384,256]{1,0:T(8,128)(2,1)} %param.7) | copy-start | bytes 589828
  33.1 48.4 %all-to-all-start = ((bf16[16,2,24576]{2,1,0:T(2,128)(2,1)}), bf16[16,2,24576]{2,1,0:T(2,128)(2,1)S(1)}, u32[]{:S(2)}, u32[]{:S(2)}) async-start(bf16[16,2,24576]{2,1,0:T(2,128)(2,1)} %reshape.58), calls=%async_computation | async-start | bytes 3145728 | tf_op jit(solution)/shard_map/all_to_all | solution.py:47
  83.6 5.7 %copy-start.4 = (s32[384]{0:T(512)S(1)}, s32[384]{0:T(512)}, u32[]{:S(2)}) copy-start(s32[384]{0:T(512)} %param.13) | copy-start | bytes 4612
  83.6 76.8 %all-to-all-start.2 = ((bf16[16,384,256]{1,2,0:T(8,128)(2,1)}), bf16[16,384,256]{1,2,0:T(8,128)(2,1)}, u32[]{:S(2)}, u32[]{:S(2)}) async-start(bf16[16,384,256]{1,2,0:T(8,128)(2,1)} %stack.2), calls=%async_computation.2 | async-start | bytes 6291456 | tf_op jit(solution)/shard_map/all_to_all | solution.py:39
  88.6 89.1 %all-gather.3.cloned.1.call-start = ((), (), s32[]{:S(2)}) async-start(), calls=%async_computation.4 | async-start | bytes 2162688 | tf_op jit(solution)/shard_map/all_gather | solution.py:43
  160.5 49.2 %all-to-all-start.1 = ((bf16[12,32,4,2,256]{4,3,2,0,1:T(2,128)(2,1)}), bf16[12,32,4,2,256]{4,3,2,0,1:T(2,128)(2,1)S(1)}, u32[]{:S(2)}, u32[]{:S(2)}) async-start(bf16[12,32,4,2,256]{4,3,2,0,1:T(2,128)(2,1)} %broadcast_select_fusion), calls=%async_computation.1 | async-start | bytes 3145728 | tf_op jit(solution)/shard_map/all_to_all | solution.py:54
  170.7 92.7 %all-gather.5.cloned.1.call-start = ((), (), s32[]{:S(2)}) async-start(), calls=%async_computation.5 | async-start | bytes 2162688 | tf_op jit(solution)/shard_map/all_gather | solution.py:46
  171.5 161.0 %reduce-scatter.2.cloned.1.call-start = ((), (), s32[]{:S(2)}) async-start(), calls=%async_computation.6 | async-start | bytes 3342336 | tf_op jit(solution)/shard_map/reduce_scatter | solution.py:73
  210.7 12.5 %collective-permute-start = (bf16[256,2,256]{2,1,0:T(2,128)(2,1)}, bf16[256,2,256]{2,1,0:T(2,128)(2,1)S(1)}, u32[]{:S(2)}, u32[]{:S(2)}) collective-permute-start(bf16[256,2,256]{2,1,0:T(2,128)(2,1)} %bitcast.6), channel_id=1, source_target_pairs={{0,16},{16,32},{32,48},{48,64},{64,80},{80,96},{96,112},{112,128},... | collective-permute-start | bytes 786440 | tf_op jit(solution)/shard_map/ppermute | solution.py:14
  223.2 0.9 copy-start.3
  267.7 0.7 copy-start.5
  267.7 1.4 copy-start
  268.3 64.2 %copy-start.2 = (bf16[384,256]{1,0:T(8,128)(2,1)S(1)}, bf16[384,256]{1,0:T(8,128)(2,1)}, u32[]{:S(2)}) copy-start(bf16[384,256]{1,0:T(8,128)(2,1)} %param.7) | copy-start | bytes 589828
Sparse Core Ops, SparseCore 0:
  92.6 85.0 all-gather.2
  180.7 82.6 all-gather.4
  267.8 64.6 reduce-scatter.1
